TPU v7x, 32 devices: a whole 2x2x4 slice. The times are simulated.
32 devices in a mesh: groups: 2 (over x), seq: 16 (over z, y, core).
Axes of the slice: x: 2, y: 2, z: 4, core: 2. Of those that a mesh axis runs over, the one named last changes fastest.
Arguments:
- video_qkv: bfloat16 [4, 1536, 3, 4096], P('groups', 'seq'), parts along dimension 0, may hold values from -48 to 48
- video_cross_q: bfloat16 [4, 1536, 4096], P('groups', 'seq'), parts along dimension 0, may hold values from -48 to 48
- audio_kv_v: bfloat16 [4, 512, 2, 4096], P('groups', 'seq'), parts along dimension 0, may hold values from -4 to 4
- audio_qkv: bfloat16 [4, 512, 3, 2048], P('groups', 'seq'), parts along dimension 0, may hold values from -48 to 48
- audio_cross_q: bfloat16 [4, 512, 2048], P('groups', 'seq'), parts along dimension 0, may hold values from -48 to 48
- video_kv_a: bfloat16 [4, 1536, 2, 2048], P('groups', 'seq'), parts along dimension 0, may hold values from -4 to 4
- audio_valid: int32 [4], P('groups'), parts along dimension 0, may hold values from 256 to 512, as said below
- branch_prompt: int32 [4], P('groups'), parts along dimension 0, may hold values from 0 to 3
- video_gate: float32 [4, 4096], replicated, may hold values from 0.5 to 1.5
- audio_gate: float32 [4, 2048], replicated, may hold values from 0.5 to 1.5
Outputs:
- video_out: bfloat16 [4, 1536, 4096], P('groups', 'seq'), parts along dimension 0
- audio_out: bfloat16 [4, 512, 2048], P('groups', 'seq'), parts along dimension 0
There are 2 independent parts, one for each index of `groups`. A program takes and returns all parts, laid end to end along the dimension named above; an argument that names none is the same for every part. Nothing has to cross between parts.
Inputs may be any that keep to these rules, and one draw needn't show every extreme that they name: `audio_valid`: at least one branch has all 512 audio tokens valid.
All inputs are finite; a program needn't handle non-finite values.
Results may differ from a plain program's by a relative error of at most 0.0058.
Values may be sent and summed in bfloat16 or wider, within the bound.
A program may use at most 128 MiB of HBM per device.

v0:
```python
import jax
import jax.numpy as jnp
from jax import lax
from jax.sharding import PartitionSpec as P

HV = 32
HA = 16
PROMPTS = 4


def block_attend(queries, key_rows, value_rows, allowed):
    scores = jnp.dot(queries, key_rows.T, preferred_element_type=jnp.float32) * queries.shape[
        -1
    ] ** (-0.5)
    if allowed is not None:
        scores = jnp.where(allowed[None, :], scores, -jnp.inf)
    row_max = jnp.max(scores, axis=1, keepdims=True)
    weights = jnp.exp(scores - row_max)
    shares = (weights / jnp.sum(weights, axis=1, keepdims=True)).astype(jnp.bfloat16)
    return jnp.dot(shares, value_rows, preferred_element_type=jnp.float32).astype(jnp.bfloat16)


def attend(queries, key_rows, value_rows, allowed):
    row_count, head_width = queries.shape
    block_rows = row_count
    while block_rows % 2 == 0 and block_rows // 2 >= 512:
        block_rows = block_rows // 2

    def one_block(block_queries):
        return block_attend(block_queries, key_rows, value_rows, allowed)

    result = lax.map(one_block, queries.reshape(row_count // block_rows, block_rows, head_width))
    return result.reshape(row_count, head_width)


def to_items(source, head_count):
    lead_count, row_count = (source.shape[0], source.shape[1])
    middle = source.shape[2:-1]
    head_width = source.shape[-1] // head_count
    result = source.reshape((lead_count, row_count) + middle + (head_count, head_width))
    axes_order = (0, len(middle) + 2, 1) + tuple(range(2, len(middle) + 2)) + (len(middle) + 3,)
    result = jnp.transpose(result, axes_order)
    return result.reshape((lead_count * head_count, row_count) + middle + (head_width,))


def from_items(source, head_count):
    item_count, row_count, head_width = source.shape
    result = source.reshape(item_count // head_count, head_count, row_count, head_width)
    return jnp.transpose(result, (0, 2, 1, 3)).reshape(
        item_count // head_count, row_count, head_count * head_width
    )


def self_items(packed):
    return attend(packed[:, 0], packed[:, 1], packed[:, 2], None)


def self_masked(packed):
    return attend(packed[0][:, 0], packed[0][:, 1], packed[0][:, 2], packed[1] > 0.5)


def cross_masked(packed):
    return attend(packed[0], packed[1][:, 0], packed[1][:, 1], packed[2] > 0.5)


def cross_items(packed):
    return attend(packed[0], packed[1][:, 0], packed[1][:, 1], None)


def local_gates(gates, head_count, item_count):
    gate_items = to_items(gates[:, None, :], head_count)[:, 0, :]
    first_item = lax.axis_index("seq") * item_count
    return lax.dynamic_slice_in_dim(gate_items, first_item, item_count, 0)


def on_device(
    video_qkv,
    video_cross_q,
    audio_kv_v,
    audio_qkv,
    audio_cross_q,
    video_kv_a,
    audio_valid,
    branch_prompt,
    video_gate,
    audio_gate,
):
    local_audio = audio_qkv.shape[1]
    positions = lax.axis_index("seq") * local_audio + jnp.arange(local_audio, dtype=jnp.int32)
    allowed_local = (positions[None, :] < audio_valid[:, None]).astype(jnp.bfloat16)
    video_items = to_items(video_qkv, HV)
    video_query = to_items(video_cross_q, HV)
    video_keys = to_items(audio_kv_v, HV)
    video_allowed = jnp.repeat(allowed_local, HV, axis=0)
    audio_items = to_items(audio_qkv, HA)
    audio_query = to_items(audio_cross_q, HA)
    audio_keys = to_items(video_kv_a, HA)
    audio_allowed = jnp.repeat(allowed_local, HA, axis=0)
    video_items, video_query, video_keys, video_allowed = (
        lax.all_to_all(video_items, "seq", split_axis=0, concat_axis=1, tiled=True),
        lax.all_to_all(video_query, "seq", split_axis=0, concat_axis=1, tiled=True),
        lax.all_to_all(video_keys, "seq", split_axis=0, concat_axis=1, tiled=True),
        lax.all_to_all(video_allowed, "seq", split_axis=0, concat_axis=1, tiled=True),
    )
    audio_items, audio_query, audio_keys, audio_allowed = (
        lax.all_to_all(audio_items, "seq", split_axis=0, concat_axis=1, tiled=True),
        lax.all_to_all(audio_query, "seq", split_axis=0, concat_axis=1, tiled=True),
        lax.all_to_all(audio_keys, "seq", split_axis=0, concat_axis=1, tiled=True),
        lax.all_to_all(audio_allowed, "seq", split_axis=0, concat_axis=1, tiled=True),
    )
    video_self = lax.map(self_items, video_items)
    video_cross = lax.map(cross_masked, (video_query, video_keys, video_allowed))
    audio_self = lax.map(self_masked, (audio_items, audio_allowed))
    audio_cross = lax.map(cross_items, (audio_query, audio_keys))
    chosen = (branch_prompt[:, None] == jnp.arange(PROMPTS, dtype=jnp.int32)[None, :]).astype(
        jnp.float32
    )
    video_gates = jnp.dot(chosen, video_gate, precision=lax.Precision.HIGHEST)
    audio_gates = jnp.dot(chosen, audio_gate, precision=lax.Precision.HIGHEST)
    video_slice = local_gates(video_gates, HV, video_self.shape[0])
    audio_slice = local_gates(audio_gates, HA, audio_self.shape[0])
    video_return = (
        video_self.astype(jnp.float32) + video_slice[:, None, :] * video_cross.astype(jnp.float32)
    ).astype(jnp.bfloat16)
    audio_return = (
        audio_self.astype(jnp.float32) + audio_slice[:, None, :] * audio_cross.astype(jnp.float32)
    ).astype(jnp.bfloat16)
    video_back, audio_back = (
        lax.all_to_all(video_return, "seq", split_axis=1, concat_axis=0, tiled=True),
        lax.all_to_all(audio_return, "seq", split_axis=1, concat_axis=0, tiled=True),
    )
    return (from_items(video_back, HV), from_items(audio_back, HA))


def solution(mesh):
    placed = (
        P("groups", "seq", None, None),
        P("groups", "seq", None),
        P("groups", "seq", None, None),
        P("groups", "seq", None, None),
        P("groups", "seq", None),
        P("groups", "seq", None, None),
        P("groups"),
        P("groups"),
        P(),
        P(),
    )
    return jax.shard_map(
        on_device,
        mesh=mesh,
        in_specs=placed,
        out_specs=(P("groups", "seq", None), P("groups", "seq", None)),
        check_vma=False,
    )
```

profile of v0, /device:TPU:13, one launch (start us, length us, event | category | flops | bytes accessed | tf_op | source)
XLA Modules:
  0.0 380.2 jit_solution(1439106227688947911)
XLA Ops:
  2.1 6.6 %all-to-all-start.5 = ((bf16[16,2,32]{2,1,0:T(2,128)(2,1)}), bf16[16,2,32]{2,1,0:T(2,128)(2,1)S(1)}, u32[]{:S(2)}, u32[]{:S(2)}) async-start(bf16[16,2,32]{2,1,0:T(2,128)(2,1)} %broadcast_in_dim.90), calls=%async_computation.5 | async-start | bytes 16384 | tf_op jit(solution)/shard_map/all_to_all | solution.py:109
  9.6 2.7 all-to-all-done.5
  13.0 6.0 %all-to-all-start.3 = ((bf16[16,4,32]{2,1,0:T(4,128)(2,1)}), bf16[16,4,32]{2,1,0:T(4,128)(2,1)S(1)}, u32[]{:S(2)}, u32[]{:S(2)}) async-start(bf16[16,4,32]{2,1,0:T(4,128)(2,1)} %broadcast_in_dim.89), calls=%async_computation.3 | async-start | bytes 32768 | tf_op jit(solution)/shard_map/all_to_all | solution.py:103
  19.8 3.4 all-to-all-done.3
  23.2 5.8 %all-to-all-start.7 = ((bf16[32,32,128]{2,1,0:T(8,128)(2,1)}), bf16[32,32,128]{2,1,0:T(8,128)(2,1)S(1)}, u32[]{:S(2)}, u32[]{:S(2)}) async-start(bf16[32,32,128]{2,1,0:T(8,128)(2,1)} %bitcast.53), calls=%async_computation.7 | async-start | bytes 524288 | tf_op jit(solution)/shard_map/all_to_all | solution.py:107
  30.3 6.7 %all-to-all-done.7 = bf16[32,32,128]{2,1,0:T(8,128)(2,1)S(1)} async-done(((bf16[32,32,128]{2,1,0:T(8,128)(2,1)}), bf16[32,32,128]{2,1,0:T(8,128)(2,1)S(1)}, u32[]{:S(2)}, u32[]{:S(2)}) %all-to-all-start.7) | async-done | bytes 262176 | tf_op jit(solution)/shard_map/all_to_all | solution.py:107
  37.7 5.6 %all-to-all-start.6 = ((bf16[32,32,3,128]{3,1,2,0:T(8,128)(2,1)}), bf16[32,32,3,128]{3,1,2,0:T(8,128)(2,1)S(1)}, u32[]{:S(2)}, u32[]{:S(2)}) async-start(bf16[32,32,3,128]{3,1,2,0:T(8,128)(2,1)} %bitcast.48), calls=%async_computation.6 | async-start | bytes 1572864 | tf_op jit(solution)/shard_map/all_to_all | solution.py:106
  45.8 16.8 %all-to-all-done.6 = bf16[32,32,3,128]{3,1,2,0:T(8,128)(2,1)S(1)} async-done(((bf16[32,32,3,128]{3,1,2,0:T(8,128)(2,1)}), bf16[32,32,3,128]{3,1,2,0:T(8,128)(2,1)S(1)}, u32[]{:S(2)}, u32[]{:S(2)}) %all-to-all-start.6) | async-done | bytes 786464 | tf_op jit(solution)/shard_map/all_to_all | solution.py:106
  62.6 4.9 %all-to-all-start.2 = ((bf16[64,32,2,128]{3,1,2,0:T(8,128)(2,1)}), bf16[64,32,2,128]{3,1,2,0:T(8,128)(2,1)S(1)}, u32[]{:S(2)}, u32[]{:S(2)}) async-start(bf16[64,32,2,128]{3,1,2,0:T(8,128)(2,1)} %bitcast.36), calls=%async_computation.2 | async-start | bytes 2097152 | tf_op jit(solution)/shard_map/all_to_all | solution.py:102
  69.9 22.5 %all-to-all-done.2 = bf16[64,32,2,128]{3,1,2,0:T(8,128)(2,1)S(1)} async-done(((bf16[64,32,2,128]{3,1,2,0:T(8,128)(2,1)}), bf16[64,32,2,128]{3,1,2,0:T(8,128)(2,1)S(1)}, u32[]{:S(2)}, u32[]{:S(2)}) %all-to-all-start.2) | async-done | bytes 1048608 | tf_op jit(solution)/shard_map/all_to_all | solution.py:102
  93.4 4.9 %all-to-all-start.1 = ((bf16[64,96,128]{2,1,0:T(8,128)(2,1)}), bf16[64,96,128]{2,1,0:T(8,128)(2,1)S(1)}, u32[]{:S(2)}, u32[]{:S(2)}) async-start(bf16[64,96,128]{2,1,0:T(8,128)(2,1)} %bitcast.30), calls=%async_computation.1 | async-start | bytes 3145728 | tf_op jit(solution)/shard_map/all_to_all | solution.py:101
  98.3 2.8 reshape.114
  102.9 31.6 %all-to-all-done.1 = bf16[64,96,128]{2,1,0:T(8,128)(2,1)S(1)} async-done(((bf16[64,96,128]{2,1,0:T(8,128)(2,1)}), bf16[64,96,128]{2,1,0:T(8,128)(2,1)S(1)}, u32[]{:S(2)}, u32[]{:S(2)}) %all-to-all-start.1) | async-done | bytes 1572896 | tf_op jit(solution)/shard_map/all_to_all | solution.py:101
  135.6 4.9 %all-to-all-start.8 = ((bf16[32,96,2,128]{3,1,2,0:T(8,128)(2,1)}), bf16[32,96,2,128]{3,1,2,0:T(8,128)(2,1)}, u32[]{:S(2)}, u32[]{:S(2)}) async-start(bf16[32,96,2,128]{3,1,2,0:T(8,128)(2,1)} %bitcast.59), calls=%async_computation.8 | async-start | bytes 3145728 | tf_op jit(solution)/shard_map/all_to_all | solution.py:108
  140.6 3.8 copy.110
  144.4 4.0 %copy.80 = bf16[2,32,96,3,128]{4,2,3,1,0:T(8,128)(2,1)} copy(bf16[2,32,96,3,128]{4,1,2,3,0:T(8,128)(2,1)S(1)} %bitcast.231) | data formatting | bytes 9437184 | tf_op jit(solution)/shard_map/transpose | solution.py:42
  154.0 22.8 %all-to-all-done.8 = bf16[32,96,2,128]{3,1,2,0:T(8,128)(2,1)} async-done(((bf16[32,96,2,128]{3,1,2,0:T(8,128)(2,1)}), bf16[32,96,2,128]{3,1,2,0:T(8,128)(2,1)}, u32[]{:S(2)}, u32[]{:S(2)}) %all-to-all-start.8) | async-done | bytes 1572896 | tf_op jit(solution)/shard_map/all_to_all | solution.py:108
  176.8 4.9 %all-to-all-start = ((bf16[64,96,3,128]{3,1,2,0:T(8,128)(2,1)}), bf16[64,96,3,128]{3,1,2,0:T(8,128)(2,1)}, u32[]{:S(2)}, u32[]{:S(2)}) async-start(bf16[64,96,3,128]{3,1,2,0:T(8,128)(2,1)} %bitcast.230), calls=%async_computation | async-start | bytes 9437184 | tf_op jit(solution)/shard_map/all_to_all | solution.py:100
  184.0 6.3 %while.73 = (s32[]{:T(128)}, bf16[2,512,128]{2,1,0:T(8,128)(2,1)}, bf16[2,512,128]{2,1,0:T(8,128)(2,1)S(1)}, bf16[2,1536,2,128]{3,1,2,0:T(8,128)(2,1)S(1)}, s32[]{:T(128)}) while((s32[]{:T(128)}, bf16[2,512,128]{2,1,0:T(8,128)(2,1)}, bf16[2,512,128]{2,1,0:T(8,128)(2,1)S(1)}, bf16[2,1536,2,128]{3,1,2,0:T(8,128)(2,1)S(1)}, s32[]{:T(128)}) %tuple.140), condition=%wide.region_19.20_spmd, body=%wide.region_16.19_spmd.sunk | while | flops 408222720 | bytes 14166153 | solution.py:114
  193.8 17.0 %while.71 = (s32[]{:T(128)}, bf16[4,1536,128]{2,1,0:T(8,128)(2,1)}, bf16[4,1536,128]{2,1,0:T(8,128)(2,1)S(1)}, bf16[4,512,2,128]{3,1,2,0:T(8,128)(2,1)}, bf16[4,...) while((s32[]{:T(128)}, bf16[4,1536,128]{2,1,0:T(8,128)(2,1)}, ...), condition=%wide.region_11.12_spmd, body=%wide.region_6.11_spmd.sunk | while | flops 204570624 | bytes 8015114 | solution.py:112
  199.1 2.4 while.75
  210.7 74.7 %all-to-all-done = bf16[64,96,3,128]{3,1,2,0:T(8,128)(2,1)} async-done(((bf16[64,96,3,128]{3,1,2,0:T(8,128)(2,1)}), bf16[64,96,3,128]{3,1,2,0:T(8,128)(2,1)}, u32[]{:S(2)}, u32[]{:S(2)}) %all-to-all-start) | async-done | bytes 4718624 | tf_op jit(solution)/shard_map/all_to_all | solution.py:100
  285.5 4.9 %all-to-all-start.9 = ((bf16[2,512,128]{2,0,1:T(2,128)(2,1)}), bf16[2,512,128]{2,0,1:T(2,128)(2,1)}, u32[]{:S(2)}, u32[]{:S(2)}) async-start(bf16[2,512,128]{2,0,1:T(2,128)(2,1)} %copy.100), calls=%async_computation.9 | async-start | bytes 524288 | tf_op jit(solution)/shard_map/all_to_all | solution.py:130
  290.4 5.6 %copy.81 = bf16[4,16,96,3,128]{4,2,1,3,0:T(8,128)(2,1)} copy(bf16[4,16,96,3,128]{4,2,3,0,1:T(8,128)(2,1)} %bitcast.27) | data formatting | bytes 9437184 | tf_op jit(solution)/shard_map/all_to_all | solution.py:100
  296.2 29.7 %while.69 = (s32[]{:T(128)}, bf16[4,1536,128]{2,1,0:T(8,128)(2,1)S(1)}, bf16[4,1536,3,128]{3,1,2,0:T(8,128)(2,1)}, s32[]{:T(128)}, s32[]{:T(128)}, /*index=5*/s32[]{:T(128)}) while((s32[]{:T(128)}, bf16[4,1536,128]{2,1,0:T(8,128)(2,1)S(1)}, bf16[4,1536,3,128]{3,1,2,0:T(8,128)(2,1)}, s32[]{:T(128)}, s32[]{:T(128)}, /*index=5*/s32[]{:T(128)}) %tuple.136), condition=%wide.region_5.6_spmd, body=%wide.region_0.5_spmd.sunk | while | flops 614693376 | bytes 20858080 | solution.py:111
  297.6 5.9 %while.74 = (s32[]{:T(128)}, bf16[2,768,128]{2,1,0:T(8,128)(2,1)S(1)}, bf16[2,768,128]{2,1,0:T(8,128)(2,1)S(1)}, bf16[1536,128]{1,0:T(8,128)(2,1)S(1)}, bf16[1536,128]{1,0:T(8,128)(2,1)S(1)}, /*index=5*/s32[]{:T(128)}) while((s32[]{:T(128)}, bf16[2,768,128]{2,1,0:T(8,128)(2,1)S(1)}, bf16[2,768,128]{2,1,0:T(8,128)(2,1)S(1)}, ...), condition=%wide.region_4.4_spmd, body=%wide.region_1.3_spmd.sunk | while | flops 614693376 | bytes 15352917 | solution.py:32
  305.1 5.9 %while.74 = (s32[]{:T(128)}, bf16[2,768,128]{2,1,0:T(8,128)(2,1)S(1)}, bf16[2,768,128]{2,1,0:T(8,128)(2,1)S(1)}, bf16[1536,128]{1,0:T(8,128)(2,1)S(1)}, bf16[1536,128]{1,0:T(8,128)(2,1)S(1)}, /*index=5*/s32[]{:T(128)}) while((s32[]{:T(128)}, bf16[2,768,128]{2,1,0:T(8,128)(2,1)S(1)}, bf16[2,768,128]{2,1,0:T(8,128)(2,1)S(1)}, ...), condition=%wide.region_4.4_spmd, body=%wide.region_1.3_spmd.sunk | while | flops 614693376 | bytes 15352917 | solution.py:32
  312.5 5.9 %while.74 = (s32[]{:T(128)}, bf16[2,768,128]{2,1,0:T(8,128)(2,1)S(1)}, bf16[2,768,128]{2,1,0:T(8,128)(2,1)S(1)}, bf16[1536,128]{1,0:T(8,128)(2,1)S(1)}, bf16[1536,128]{1,0:T(8,128)(2,1)S(1)}, /*index=5*/s32[]{:T(128)}) while((s32[]{:T(128)}, bf16[2,768,128]{2,1,0:T(8,128)(2,1)S(1)}, bf16[2,768,128]{2,1,0:T(8,128)(2,1)S(1)}, ...), condition=%wide.region_4.4_spmd, body=%wide.region_1.3_spmd.sunk | while | flops 614693376 | bytes 15352917 | solution.py:32
  319.9 5.9 %while.74 = (s32[]{:T(128)}, bf16[2,768,128]{2,1,0:T(8,128)(2,1)S(1)}, bf16[2,768,128]{2,1,0:T(8,128)(2,1)S(1)}, bf16[1536,128]{1,0:T(8,128)(2,1)S(1)}, bf16[1536,128]{1,0:T(8,128)(2,1)S(1)}, /*index=5*/s32[]{:T(128)}) while((s32[]{:T(128)}, bf16[2,768,128]{2,1,0:T(8,128)(2,1)S(1)}, bf16[2,768,128]{2,1,0:T(8,128)(2,1)S(1)}, ...), condition=%wide.region_4.4_spmd, body=%wide.region_1.3_spmd.sunk | while | flops 614693376 | bytes 15352917 | solution.py:32
  327.8 8.2 %copy.88 = bf16[4,1536,128]{2,0,1:T(4,128)(2,1)} copy(bf16[4,1536,128]{2,1,0:T(8,128)(2,1)S(1)} %add_convert_fusion) | data formatting | bytes 3145728 | tf_op jit(solution)/shard_map/convert_element_type | solution.py:124
  336.0 6.0 %all-to-all-start.4 = ((bf16[4,1536,128]{2,0,1:T(4,128)(2,1)}), bf16[4,1536,128]{2,0,1:T(4,128)(2,1)S(1)}, u32[]{:S(2)}, u32[]{:S(2)}) async-start(bf16[4,1536,128]{2,0,1:T(4,128)(2,1)} %copy.88), calls=%async_computation.4 | async-start | bytes 3145728 | tf_op jit(solution)/shard_map/all_to_all | solution.py:129
  343.8 34.4 %all-to-all-done.4 = bf16[4,1536,128]{2,0,1:T(4,128)(2,1)S(1)} async-done(((bf16[4,1536,128]{2,0,1:T(4,128)(2,1)}), bf16[4,1536,128]{2,0,1:T(4,128)(2,1)S(1)}, u32[]{:S(2)}, u32[]{:S(2)}) %all-to-all-start.4) | async-done | bytes 1572896 | tf_op jit(solution)/shard_map/all_to_all | solution.py:129
  (197 shorter events, 93.1 us)
Async XLA Ops:
  0.6 147.7 %copy-start = (f32[4,4096]{1,0:T(4,128)S(1)}, f32[4,4096]{1,0:T(4,128)}, u32[]{:S(2)}) copy-start(f32[4,4096]{1,0:T(4,128)} %param.30) | copy-start | bytes 196612
  0.6 28.4 %copy-start.15 = (bf16[2,32,3,2048]{3,1,2,0:T(8,128)(2,1)S(1)}, bf16[2,32,3,2048]{3,1,2,0:T(8,128)(2,1)}, u32[]{:S(2)}) copy-start(bf16[2,32,3,2048]{3,1,2,0:T(8,128)(2,1)} %param.25) | copy-start | bytes 2359300
  2.1 10.3 %all-to-all-start.5 = ((bf16[16,2,32]{2,1,0:T(2,128)(2,1)}), bf16[16,2,32]{2,1,0:T(2,128)(2,1)S(1)}, u32[]{:S(2)}, u32[]{:S(2)}) async-start(bf16[16,2,32]{2,1,0:T(2,128)(2,1)} %broadcast_in_dim.90), calls=%async_computation.5 | async-start | bytes 16384 | tf_op jit(solution)/shard_map/all_to_all | solution.py:109
  13.0 10.2 %all-to-all-start.3 = ((bf16[16,4,32]{2,1,0:T(4,128)(2,1)}), bf16[16,4,32]{2,1,0:T(4,128)(2,1)S(1)}, u32[]{:S(2)}, u32[]{:S(2)}) async-start(bf16[16,4,32]{2,1,0:T(4,128)(2,1)} %broadcast_in_dim.89), calls=%async_computation.3 | async-start | bytes 32768 | tf_op jit(solution)/shard_map/all_to_all | solution.py:103
  23.2 13.8 %all-to-all-start.7 = ((bf16[32,32,128]{2,1,0:T(8,128)(2,1)}), bf16[32,32,128]{2,1,0:T(8,128)(2,1)S(1)}, u32[]{:S(2)}, u32[]{:S(2)}) async-start(bf16[32,32,128]{2,1,0:T(8,128)(2,1)} %bitcast.53), calls=%async_computation.7 | async-start | bytes 524288 | tf_op jit(solution)/shard_map/all_to_all | solution.py:107
  29.2 14.2 %copy-start.9 = (bf16[2,32,2,4096]{3,2,1,0:T(2,128)(2,1)S(1)}, bf16[2,32,2,4096]{3,2,1,0:T(2,128)(2,1)}, u32[]{:S(2)}) copy-start(bf16[2,32,2,4096]{3,2,1,0:T(2,128)(2,1)} %param.24) | copy-start | bytes 3145732
  37.0 0.7 copy-start.10
  37.7 24.9 %all-to-all-start.6 = ((bf16[32,32,3,128]{3,1,2,0:T(8,128)(2,1)}), bf16[32,32,3,128]{3,1,2,0:T(8,128)(2,1)S(1)}, u32[]{:S(2)}, u32[]{:S(2)}) async-start(bf16[32,32,3,128]{3,1,2,0:T(8,128)(2,1)} %bitcast.48), calls=%async_computation.6 | async-start | bytes 1572864 | tf_op jit(solution)/shard_map/all_to_all | solution.py:106
  45.8 21.7 %copy-start.8 = (bf16[2,96,4096]{2,1,0:T(8,128)(2,1)S(1)}, bf16[2,96,4096]{2,1,0:T(8,128)(2,1)}, u32[]{:S(2)}) copy-start(bf16[2,96,4096]{2,1,0:T(8,128)(2,1)} %param.23) | copy-start | bytes 4718596
  62.6 5.3 %copy-start.6 = (bf16[32,32,3,128]{3,1,2,0:T(8,128)(2,1)}, bf16[32,32,3,128]{3,1,2,0:T(8,128)(2,1)S(1)}, u32[]{:S(2)}) copy-start(bf16[32,32,3,128]{3,1,2,0:T(8,128)(2,1)S(1)} %all-to-all-done.6) | copy-start | bytes 2359300
  62.6 29.8 %all-to-all-start.2 = ((bf16[64,32,2,128]{3,1,2,0:T(8,128)(2,1)}), bf16[64,32,2,128]{3,1,2,0:T(8,128)(2,1)S(1)}, u32[]{:S(2)}, u32[]{:S(2)}) async-start(bf16[64,32,2,128]{3,1,2,0:T(8,128)(2,1)} %bitcast.36), calls=%async_computation.2 | async-start | bytes 2097152 | tf_op jit(solution)/shard_map/all_to_all | solution.py:102
  92.4 1.0 copy-start.4
  93.4 41.1 %all-to-all-start.1 = ((bf16[64,96,128]{2,1,0:T(8,128)(2,1)}), bf16[64,96,128]{2,1,0:T(8,128)(2,1)S(1)}, u32[]{:S(2)}, u32[]{:S(2)}) async-start(bf16[64,96,128]{2,1,0:T(8,128)(2,1)} %bitcast.30), calls=%async_computation.1 | async-start | bytes 3145728 | tf_op jit(solution)/shard_map/all_to_all | solution.py:101
  134.5 1.1 copy-start.2
  135.6 41.2 %all-to-all-start.8 = ((bf16[32,96,2,128]{3,1,2,0:T(8,128)(2,1)}), bf16[32,96,2,128]{3,1,2,0:T(8,128)(2,1)}, u32[]{:S(2)}, u32[]{:S(2)}) async-start(bf16[32,96,2,128]{3,1,2,0:T(8,128)(2,1)} %bitcast.59), calls=%async_computation.8 | async-start | bytes 3145728 | tf_op jit(solution)/shard_map/all_to_all | solution.py:108
  144.3 4.0 %copy-start.17 = (s32[2]{0:T(128)S(1)}, s32[2]{0:T(128)}, u32[]{:S(2)}) copy-start(s32[2]{0:T(128)} %param.29) | copy-start | bytes 28
  144.4 4.3 %copy-start.18 = (f32[4,2048]{1,0:T(4,128)S(1)}, f32[4,2048]{1,0:T(4,128)}, u32[]{:S(2)}) copy-start(f32[4,2048]{1,0:T(4,128)} %param.31) | copy-start | bytes 98308
  144.4 5.4 %copy-start.11 = (bf16[32,32,128]{2,1,0:T(8,128)(2,1)S(1)}, bf16[32,32,128]{2,1,0:T(8,128)(2,1)}, u32[]{:S(2)}) copy-start(bf16[32,32,128]{2,1,0:T(8,128)(2,1)} %copy-done.10) | copy-start | bytes 786436
  144.4 5.4 %copy-start.7 = (bf16[32,32,3,128]{3,1,2,0:T(8,128)(2,1)S(1)}, bf16[32,32,3,128]{3,1,2,0:T(8,128)(2,1)}, u32[]{:S(2)}) copy-start(bf16[32,32,3,128]{3,1,2,0:T(8,128)(2,1)} %copy-done.6) | copy-start | bytes 2359300
  149.9 2.1 copy-start.5
  152.0 2.0 copy-start.12
  152.0 1.9 copy-start.3
  176.8 108.6 %all-to-all-start = ((bf16[64,96,3,128]{3,1,2,0:T(8,128)(2,1)}), bf16[64,96,3,128]{3,1,2,0:T(8,128)(2,1)}, u32[]{:S(2)}, u32[]{:S(2)}) async-start(bf16[64,96,3,128]{3,1,2,0:T(8,128)(2,1)} %bitcast.230), calls=%async_computation | async-start | bytes 9437184 | tf_op jit(solution)/shard_map/all_to_all | solution.py:100
  184.8 1.0 copy-start.13
  186.5 0.7 copy-start.14
  187.9 1.0 copy-start.13
  189.6 0.7 copy-start.14
  285.5 50.6 %all-to-all-start.9 = ((bf16[2,512,128]{2,0,1:T(2,128)(2,1)}), bf16[2,512,128]{2,0,1:T(2,128)(2,1)}, u32[]{:S(2)}, u32[]{:S(2)}) async-start(bf16[2,512,128]{2,0,1:T(2,128)(2,1)} %copy.100), calls=%async_computation.9 | async-start | bytes 524288 | tf_op jit(solution)/shard_map/all_to_all | solution.py:130
  296.2 29.7 %copy-start.16 = (f32[4,128]{1,0:T(4,128)S(1)}, f32[4,128]{1,0:T(4,128)}, u32[]{:S(2)}) copy-start(f32[4,128]{1,0:T(4,128)} %constant_dynamic-slice_fusion.2) | copy-start | bytes 6148
  336.0 42.2 %all-to-all-start.4 = ((bf16[4,1536,128]{2,0,1:T(4,128)(2,1)}), bf16[4,1536,128]{2,0,1:T(4,128)(2,1)S(1)}, u32[]{:S(2)}, u32[]{:S(2)}) async-start(bf16[4,1536,128]{2,0,1:T(4,128)(2,1)} %copy.88), calls=%async_computation.4 | async-start | bytes 3145728 | tf_op jit(solution)/shard_map/all_to_all | solution.py:129
  378.6 1.6 copy-start.1
where the time goes:
time: 382 us; the launch traced here: 380 us
  waiting for transfers between devices  216 us (57%)
  local copies, waits for them, and re-layouts  65 us (17%)
  starting transfers between devices  54.7 us (14%)
  matrix products  28.3 us (7%)
  other arithmetic  14.8 us (4%)
    all_to_all x1, waiting for transfers between devices, on_device(): lax.all_to_all(video_items, 'seq', split_axis=0, concat_axis=1, tiled=True)  74.7 us
    all_to_all x1, waiting for transfers between devices, on_device(): lax.all_to_all(video_return, 'seq', split_axis=1, concat_axis=0, tiled=True)  34.4 us
    all_to_all x1, waiting for transfers between devices, on_device(): lax.all_to_all(video_query, 'seq', split_axis=0, concat_axis=1, tiled=True)  31.6 us
    all_to_all x1, waiting for transfers between devices, on_device(): lax.all_to_all(audio_keys, 'seq', split_axis=0, concat_axis=1, tiled=True)  22.8 us
    all_to_all x1, waiting for transfers between devices, on_device(): lax.all_to_all(video_keys, 'seq', split_axis=0, concat_axis=1, tiled=True)  22.5 us
    all_to_all x1, waiting for transfers between devices, on_device(): lax.all_to_all(audio_items, 'seq', split_axis=0, concat_axis=1, tiled=True)  16.8 us
    dot_general x20, matrix products, block_attend(): jnp.dot(shares, value_rows, preferred_element_type=jnp.float32)  16 us
    dot_general x20, matrix products, block_attend(): jnp.dot(queries, key_rows.T, preferred_element_type=jnp.float32)  11.8 us
  transfers between devices with their start and end apart: 10, of which 9 were waited for; matrix products, arithmetic and copies ran while one was open for 26% of the time, Pallas kernels for 0%

commit v1 on v0

--- a/solution.py
+++ b/solution.py
@@ -6,6 +6,29 @@
 HV = 32
 HA = 16
 PROMPTS = 4
+
+
+def split_up(array, dim, length):
+    shape = array.shape
+    tiles = array.reshape(*shape[:dim], length, shape[dim] // length, *shape[dim + 1 :])
+    return jnp.moveaxis(tiles, dim, 0)
+
+
+def in_order(pieces, dim):
+    dims = list(pieces.shape[1:])
+    dims[dim] *= pieces.shape[0]
+    return jnp.moveaxis(pieces, 0, dim).reshape(dims)
+
+
+def exchange_in_pairs(shard, axis, split_dim, concat_dim):
+    size, index = (lax.axis_size(axis), lax.axis_index(axis))
+    tiles = split_up(shard, split_dim, size)
+    done = [tiles[index]]
+    for turn in range(1, size):
+        sent = tiles[index ^ turn]
+        done.append(lax.ppermute(sent, axis, [(i, i ^ turn) for i in range(size)]))
+    tiles = jnp.stack(done)[index ^ jnp.arange(size)]
+    return in_order(tiles, concat_dim)
 
 
 def block_attend(queries, key_rows, value_rows, allowed):
@@ -105,7 +128,7 @@
     audio_items, audio_query, audio_keys, audio_allowed = (
         lax.all_to_all(audio_items, "seq", split_axis=0, concat_axis=1, tiled=True),
         lax.all_to_all(audio_query, "seq", split_axis=0, concat_axis=1, tiled=True),
-        lax.all_to_all(audio_keys, "seq", split_axis=0, concat_axis=1, tiled=True),
+        exchange_in_pairs(audio_keys, "seq", 0, 1),
         lax.all_to_all(audio_allowed, "seq", split_axis=0, concat_axis=1, tiled=True),
     )
     video_self = lax.map(self_items, video_items)

time: 382 us -> 386 us (1.010)
  waiting for transfers between devices: 216 us -> 188 us
  starting transfers between devices: 54.7 us -> 76.6 us
  local copies, waits for them, and re-layouts: 65 us -> 75.5 us
    ppermute x0 -> x15, waiting for transfers between devices: none -> 37.5 us  [exchange_in_pairs(): done.append(lax.ppermute(sent, axis, [(i, i ^ turn) for i in range(size)]))]
    all_to_all x1 -> x0, waiting for transfers between devices: 22.8 us -> none  [on_device(): lax.all_to_all(audio_keys, 'seq', split_axis=0, concat_axis=1, tiled=True)]
    all_to_all x1, waiting for transfers between devices: 22.5 us -> 0.01 us  [on_device(): lax.all_to_all(video_keys, 'seq', split_axis=0, concat_axis=1, tiled=True)]
    ppermute x0 -> x15, starting transfers between devices: none -> 19.5 us  [exchange_in_pairs(): done.append(lax.ppermute(sent, axis, [(i, i ^ turn) for i in range(size)]))]
    all_to_all x1, waiting for transfers between devices: 16.8 us -> 0.5 us  [on_device(): lax.all_to_all(audio_items, 'seq', split_axis=0, concat_axis=1, tiled=True)]
    all_to_all x1, waiting for transfers between devices: 74.7 us -> 85.3 us  [on_device(): lax.all_to_all(video_items, 'seq', split_axis=0, concat_axis=1, tiled=True)]
    all_to_all x1, waiting for transfers between devices: 31.6 us -> 22.4 us  [on_device(): lax.all_to_all(video_query, 'seq', split_axis=0, concat_axis=1, tiled=True)]
    all_to_all x1, starting transfers between devices: 4.93 us -> 12.7 us  [on_device(): lax.all_to_all(video_keys, 'seq', split_axis=0, concat_axis=1, tiled=True)]
  transfers between devices with their start and end apart: 10 -> 24, of which waited for: 9 -> 11; matrix products, arithmetic and copies ran while one was open for 26% -> 28% of each run, Pallas kernels for 0% -> 0%
where the time goes in v1:
time: 386 us; the launch traced here: 384 us
  waiting for transfers between devices  188 us (49%)
  starting transfers between devices  76.6 us (20%)
  local copies, waits for them, and re-layouts  75.5 us (20%)
  matrix products  28.3 us (7%)
  other arithmetic  13.1 us (3%)
    all_to_all x1, waiting for transfers between devices, on_device(): lax.all_to_all(video_items, 'seq', split_axis=0, concat_axis=1, tiled=True)  85.3 us
    ppermute x15, waiting for transfers between devices, exchange_in_pairs(): done.append(lax.ppermute(sent, axis, [(i, i ^ turn) for i in range(size)]))  37.5 us
    all_to_all x1, waiting for transfers between devices, on_device(): lax.all_to_all(video_return, 'seq', split_axis=1, concat_axis=0, tiled=True)  34.4 us
    all_to_all x1, waiting for transfers between devices, on_device(): lax.all_to_all(video_query, 'seq', split_axis=0, concat_axis=1, tiled=True)  22.4 us
    ppermute x15, starting transfers between devices, exchange_in_pairs(): done.append(lax.ppermute(sent, axis, [(i, i ^ turn) for i in range(size)]))  19.5 us
    unnamed x58, local copies, waits for them, and re-layouts  16.4 us
    dot_general x20, matrix products, block_attend(): jnp.dot(shares, value_rows, preferred_element_type=jnp.float32)  15.9 us
    all_to_all x1, starting transfers between devices, on_device(): lax.all_to_all(video_keys, 'seq', split_axis=0, concat_axis=1, tiled=True)  12.7 us
  transfers between devices with their start and end apart: 24, of which 11 were waited for; matrix products, arithmetic and copies ran while one was open for 28% of the time, Pallas kernels for 0%

profile of v1, /device:TPU:13, one launch (start us, length us, event | category | flops | bytes accessed | tf_op | source)
XLA Modules:
  0.0 383.7 jit_solution(12361532788773907750)
XLA Ops:
  0.7 2.8 reshape.138
  10.4 6.0 %all-to-all-start.5 = ((bf16[16,2,32]{2,1,0:T(2,128)(2,1)}), bf16[16,2,32]{2,1,0:T(2,128)(2,1)S(1)}, u32[]{:S(2)}, u32[]{:S(2)}) async-start(bf16[16,2,32]{2,1,0:T(2,128)(2,1)} %broadcast_in_dim.91), calls=%async_computation.5 | async-start | bytes 16384 | tf_op jit(solution)/shard_map/all_to_all | solution.py:132
  20.7 6.0 %all-to-all-start.3 = ((bf16[16,4,32]{2,1,0:T(4,128)(2,1)}), bf16[16,4,32]{2,1,0:T(4,128)(2,1)S(1)}, u32[]{:S(2)}, u32[]{:S(2)}) async-start(bf16[16,4,32]{2,1,0:T(4,128)(2,1)} %broadcast_in_dim.90), calls=%async_computation.3 | async-start | bytes 32768 | tf_op jit(solution)/shard_map/all_to_all | solution.py:126
  32.3 3.8 copy.110
  36.1 4.0 %copy.80 = bf16[2,32,96,3,128]{4,2,3,1,0:T(8,128)(2,1)} copy(bf16[2,32,96,3,128]{4,1,2,3,0:T(8,128)(2,1)S(1)} %bitcast.291) | data formatting | bytes 9437184 | tf_op jit(solution)/shard_map/transpose | solution.py:65
  42.2 6.2 %all-to-all-start.7 = ((bf16[32,32,128]{2,1,0:T(8,128)(2,1)}), bf16[32,32,128]{2,1,0:T(8,128)(2,1)S(1)}, u32[]{:S(2)}, u32[]{:S(2)}) async-start(bf16[32,32,128]{2,1,0:T(8,128)(2,1)} %bitcast.53), calls=%async_computation.7 | async-start | bytes 524288 | tf_op jit(solution)/shard_map/all_to_all | solution.py:130
  49.3 7.1 %all-to-all-done.7 = bf16[32,32,128]{2,1,0:T(8,128)(2,1)S(1)} async-done(((bf16[32,32,128]{2,1,0:T(8,128)(2,1)}), bf16[32,32,128]{2,1,0:T(8,128)(2,1)S(1)}, u32[]{:S(2)}, u32[]{:S(2)}) %all-to-all-start.7) | async-done | bytes 262176 | tf_op jit(solution)/shard_map/all_to_all | solution.py:130
  56.4 5.6 %all-to-all-start.6 = ((bf16[32,32,3,128]{3,1,2,0:T(8,128)(2,1)}), bf16[32,32,3,128]{3,1,2,0:T(8,128)(2,1)S(1)}, u32[]{:S(2)}, u32[]{:S(2)}) async-start(bf16[32,32,3,128]{3,1,2,0:T(8,128)(2,1)} %bitcast.48), calls=%async_computation.6 | async-start | bytes 1572864 | tf_op jit(solution)/shard_map/all_to_all | solution.py:129
  63.2 2.9 collective-permute-start.6
  74.6 4.0 %collective-permute-done.5 = bf16[2,96,2,128]{3,1,2,0:T(8,128)(2,1)S(1)} collective-permute-done((bf16[2,96,2,128]{3,1,2,0:T(8,128)(2,1)}, bf16[2,96,2,128]{3,1,2,0:T(8,128)(2,1)S(1)}, u32[]{:S(2)}, u32[]{:S(2)}) %collective-permute-start.5) | collective-permute-done | bytes 98336 | tf_op jit(solution)/shard_map/ppermute | solution.py:29
  78.6 2.9 collective-permute-start.10
  82.1 12.7 %all-to-all-start.2 = ((bf16[64,32,2,128]{3,1,2,0:T(8,128)(2,1)}), bf16[64,32,2,128]{3,1,2,0:T(8,128)(2,1)}, u32[]{:S(2)}, u32[]{:S(2)}) async-start(bf16[64,32,2,128]{3,1,2,0:T(8,128)(2,1)} %bitcast.36), calls=%async_computation.2 | async-start | bytes 2097152 | tf_op jit(solution)/shard_map/all_to_all | solution.py:125
  104.0 27.0 %collective-permute-done.11 = bf16[2,96,2,128]{3,1,2,0:T(8,128)(2,1)S(1)} collective-permute-done((bf16[2,96,2,128]{3,1,2,0:T(8,128)(2,1)S(1)}, bf16[2,96,2,128]{3,1,2,0:T(8,128)(2,1)S(1)}, u32[]{:S(2)}, u32[]{:S(2)}) %collective-permute-start.11) | collective-permute-done | bytes 98336 | tf_op jit(solution)/shard_map/ppermute | solution.py:29
  131.1 3.0 collective-permute-done.12
  139.4 4.1 %all-to-all-start.1 = ((bf16[64,96,128]{2,1,0:T(8,128)(2,1)}), bf16[64,96,128]{2,1,0:T(8,128)(2,1)S(1)}, u32[]{:S(2)}, u32[]{:S(2)}) async-start(bf16[64,96,128]{2,1,0:T(8,128)(2,1)} %bitcast.30), calls=%async_computation.1 | async-start | bytes 3145728 | tf_op jit(solution)/shard_map/all_to_all | solution.py:124
  144.3 6.3 %while.73 = (s32[]{:T(128)}, bf16[2,512,128]{2,1,0:T(8,128)(2,1)}, bf16[2,512,128]{2,1,0:T(8,128)(2,1)S(1)}, bf16[2,1536,2,128]{3,1,2,0:T(8,128)(2,1)S(1)}, s32[]{:T(128)}) while((s32[]{:T(128)}, bf16[2,512,128]{2,1,0:T(8,128)(2,1)}, bf16[2,512,128]{2,1,0:T(8,128)(2,1)S(1)}, bf16[2,1536,2,128]{3,1,2,0:T(8,128)(2,1)S(1)}, s32[]{:T(128)}) %tuple.156), condition=%wide.region_19.20_spmd, body=%wide.region_16.19_spmd.sunk | while | flops 408222720 | bytes 14166153 | solution.py:137
  157.3 22.4 %all-to-all-done.1 = bf16[64,96,128]{2,1,0:T(8,128)(2,1)S(1)} async-done(((bf16[64,96,128]{2,1,0:T(8,128)(2,1)}), bf16[64,96,128]{2,1,0:T(8,128)(2,1)S(1)}, u32[]{:S(2)}, u32[]{:S(2)}) %all-to-all-start.1) | async-done | bytes 1572896 | tf_op jit(solution)/shard_map/all_to_all | solution.py:124
  179.7 5.5 %all-to-all-start = ((bf16[64,96,3,128]{3,1,2,0:T(8,128)(2,1)}), bf16[64,96,3,128]{3,1,2,0:T(8,128)(2,1)}, u32[]{:S(2)}, u32[]{:S(2)}) async-start(bf16[64,96,3,128]{3,1,2,0:T(8,128)(2,1)} %bitcast.290), calls=%async_computation | async-start | bytes 9437184 | tf_op jit(solution)/shard_map/all_to_all | solution.py:123
  186.7 17.0 %while.71 = (s32[]{:T(128)}, bf16[4,1536,128]{2,1,0:T(8,128)(2,1)}, bf16[4,1536,128]{2,1,0:T(8,128)(2,1)S(1)}, bf16[4,512,2,128]{3,1,2,0:T(8,128)(2,1)}, bf16[4,...) while((s32[]{:T(128)}, bf16[4,1536,128]{2,1,0:T(8,128)(2,1)}, ...), condition=%wide.region_11.12_spmd, body=%wide.region_6.11_spmd.sunk | while | flops 204570624 | bytes 8015114 | solution.py:135
  187.8 2.4 while.75
  196.3 2.4 while.75
  203.7 85.3 %all-to-all-done = bf16[64,96,3,128]{3,1,2,0:T(8,128)(2,1)} async-done(((bf16[64,96,3,128]{3,1,2,0:T(8,128)(2,1)}), bf16[64,96,3,128]{3,1,2,0:T(8,128)(2,1)}, u32[]{:S(2)}, u32[]{:S(2)}) %all-to-all-start) | async-done | bytes 4718624 | tf_op jit(solution)/shard_map/all_to_all | solution.py:123
  288.9 4.9 %all-to-all-start.8 = ((bf16[2,512,128]{2,0,1:T(2,128)(2,1)}), bf16[2,512,128]{2,0,1:T(2,128)(2,1)}, u32[]{:S(2)}, u32[]{:S(2)}) async-start(bf16[2,512,128]{2,0,1:T(2,128)(2,1)} %copy.100), calls=%async_computation.8 | async-start | bytes 524288 | tf_op jit(solution)/shard_map/all_to_all | solution.py:153
  293.9 5.6 %copy.81 = bf16[4,16,96,3,128]{4,2,1,3,0:T(8,128)(2,1)} copy(bf16[4,16,96,3,128]{4,2,3,0,1:T(8,128)(2,1)} %bitcast.27) | data formatting | bytes 9437184 | tf_op jit(solution)/shard_map/all_to_all | solution.py:123
  299.7 29.7 %while.69 = (s32[]{:T(128)}, bf16[4,1536,128]{2,1,0:T(8,128)(2,1)S(1)}, bf16[4,1536,3,128]{3,1,2,0:T(8,128)(2,1)}, s32[]{:T(128)}, s32[]{:T(128)}, /*index=5*/s32[]{:T(128)}) while((s32[]{:T(128)}, bf16[4,1536,128]{2,1,0:T(8,128)(2,1)S(1)}, bf16[4,1536,3,128]{3,1,2,0:T(8,128)(2,1)}, s32[]{:T(128)}, s32[]{:T(128)}, /*index=5*/s32[]{:T(128)}) %tuple.151), condition=%wide.region_5.6_spmd, body=%wide.region_0.5_spmd.sunk | while | flops 614693376 | bytes 20858080 | solution.py:134
  301.1 5.9 %while.74 = (s32[]{:T(128)}, bf16[2,768,128]{2,1,0:T(8,128)(2,1)S(1)}, bf16[2,768,128]{2,1,0:T(8,128)(2,1)S(1)}, bf16[1536,128]{1,0:T(8,128)(2,1)S(1)}, bf16[1536,128]{1,0:T(8,128)(2,1)S(1)}, /*index=5*/s32[]{:T(128)}) while((s32[]{:T(128)}, bf16[2,768,128]{2,1,0:T(8,128)(2,1)S(1)}, bf16[2,768,128]{2,1,0:T(8,128)(2,1)S(1)}, ...), condition=%wide.region_4.4_spmd, body=%wide.region_1.3_spmd.sunk | while | flops 614693376 | bytes 15352917 | solution.py:55
  308.6 5.9 %while.74 = (s32[]{:T(128)}, bf16[2,768,128]{2,1,0:T(8,128)(2,1)S(1)}, bf16[2,768,128]{2,1,0:T(8,128)(2,1)S(1)}, bf16[1536,128]{1,0:T(8,128)(2,1)S(1)}, bf16[1536,128]{1,0:T(8,128)(2,1)S(1)}, /*index=5*/s32[]{:T(128)}) while((s32[]{:T(128)}, bf16[2,768,128]{2,1,0:T(8,128)(2,1)S(1)}, bf16[2,768,128]{2,1,0:T(8,128)(2,1)S(1)}, ...), condition=%wide.region_4.4_spmd, body=%wide.region_1.3_spmd.sunk | while | flops 614693376 | bytes 15352917 | solution.py:55
  316.0 5.9 %while.74 = (s32[]{:T(128)}, bf16[2,768,128]{2,1,0:T(8,128)(2,1)S(1)}, bf16[2,768,128]{2,1,0:T(8,128)(2,1)S(1)}, bf16[1536,128]{1,0:T(8,128)(2,1)S(1)}, bf16[1536,128]{1,0:T(8,128)(2,1)S(1)}, /*index=5*/s32[]{:T(128)}) while((s32[]{:T(128)}, bf16[2,768,128]{2,1,0:T(8,128)(2,1)S(1)}, bf16[2,768,128]{2,1,0:T(8,128)(2,1)S(1)}, ...), condition=%wide.region_4.4_spmd, body=%wide.region_1.3_spmd.sunk | while | flops 614693376 | bytes 15352917 | solution.py:55
  323.4 5.9 %while.74 = (s32[]{:T(128)}, bf16[2,768,128]{2,1,0:T(8,128)(2,1)S(1)}, bf16[2,768,128]{2,1,0:T(8,128)(2,1)S(1)}, bf16[1536,128]{1,0:T(8,128)(2,1)S(1)}, bf16[1536,128]{1,0:T(8,128)(2,1)S(1)}, /*index=5*/s32[]{:T(128)}) while((s32[]{:T(128)}, bf16[2,768,128]{2,1,0:T(8,128)(2,1)S(1)}, bf16[2,768,128]{2,1,0:T(8,128)(2,1)S(1)}, ...), condition=%wide.region_4.4_spmd, body=%wide.region_1.3_spmd.sunk | while | flops 614693376 | bytes 15352917 | solution.py:55
  331.3 8.2 %copy.88 = bf16[4,1536,128]{2,0,1:T(4,128)(2,1)} copy(bf16[4,1536,128]{2,1,0:T(8,128)(2,1)S(1)} %add_convert_fusion) | data formatting | bytes 3145728 | tf_op jit(solution)/shard_map/convert_element_type | solution.py:147
  339.5 6.0 %all-to-all-start.4 = ((bf16[4,1536,128]{2,0,1:T(4,128)(2,1)}), bf16[4,1536,128]{2,0,1:T(4,128)(2,1)S(1)}, u32[]{:S(2)}, u32[]{:S(2)}) async-start(bf16[4,1536,128]{2,0,1:T(4,128)(2,1)} %copy.88), calls=%async_computation.4 | async-start | bytes 3145728 | tf_op jit(solution)/shard_map/all_to_all | solution.py:152
  347.3 34.4 %all-to-all-done.4 = bf16[4,1536,128]{2,0,1:T(4,128)(2,1)S(1)} async-done(((bf16[4,1536,128]{2,0,1:T(4,128)(2,1)}), bf16[4,1536,128]{2,0,1:T(4,128)(2,1)S(1)}, u32[]{:S(2)}, u32[]{:S(2)}) %all-to-all-start.4) | async-done | bytes 1572896 | tf_op jit(solution)/shard_map/all_to_all | solution.py:152
  (250 shorter events, 117.9 us)
Async XLA Ops:
  5.6 56.6 %collective-permute-start = (bf16[2,96,2,128]{3,1,2,0:T(8,128)(2,1)}, bf16[2,96,2,128]{3,1,2,0:T(8,128)(2,1)}, u32[]{:S(2)}, u32[]{:S(2)}) collective-permute-start(bf16[2,96,2,128]{3,1,2,0:T(8,128)(2,1)} %get-tuple-element.267), channel_id=1, source_target_pairs={{0,1},{1,0},{2,3},{3,2},{4,5},{5,4},{6,7},{7,6},{8,9},{9,8},{10,11... | collective-permute-start | bytes 294920 | tf_op jit(solution)/shard_map/ppermute | solution.py:29
  6.2 57.0 %collective-permute-start.1 = (bf16[2,96,2,128]{3,1,2,0:T(8,128)(2,1)}, bf16[2,96,2,128]{3,1,2,0:T(8,128)(2,1)}, u32[]{:S(2)}, u32[]{:S(2)}) collective-permute-start(bf16[2,96,2,128]{3,1,2,0:T(8,128)(2,1)} %get-tuple-element.266), channel_id=1, source_target_pairs={{0,2},{1,3},{2,0},{3,1},{4,6},{5,7},{6,4},{7,5},{8,10},{9,11},{10,... | collective-permute-start | bytes 294920 | tf_op jit(solution)/shard_map/ppermute | solution.py:29
  6.5 60.6 %collective-permute-start.2 = (bf16[2,96,2,128]{3,1,2,0:T(8,128)(2,1)}, bf16[2,96,2,128]{3,1,2,0:T(8,128)(2,1)}, u32[]{:S(2)}, u32[]{:S(2)}) collective-permute-start(bf16[2,96,2,128]{3,1,2,0:T(8,128)(2,1)} %get-tuple-element.265), channel_id=1, source_target_pairs={{0,3},{1,2},{2,1},{3,0},{4,7},{5,6},{6,5},{7,4},{8,11},{9,10},{10,... | collective-permute-start | bytes 294920 | tf_op jit(solution)/shard_map/ppermute | solution.py:29
  7.9 62.3 %collective-permute-start.3 = (bf16[2,96,2,128]{3,1,2,0:T(8,128)(2,1)}, bf16[2,96,2,128]{3,1,2,0:T(8,128)(2,1)}, u32[]{:S(2)}, u32[]{:S(2)}) collective-permute-start(bf16[2,96,2,128]{3,1,2,0:T(8,128)(2,1)} %get-tuple-element.264), channel_id=1, source_target_pairs={{0,4},{1,5},{2,6},{3,7},{4,0},{5,1},{6,2},{7,3},{8,12},{9,13},{10,... | collective-permute-start | bytes 294920 | tf_op jit(solution)/shard_map/ppermute | solution.py:29
  8.1 63.4 %collective-permute-start.4 = (bf16[2,96,2,128]{3,1,2,0:T(8,128)(2,1)}, bf16[2,96,2,128]{3,1,2,0:T(8,128)(2,1)}, u32[]{:S(2)}, u32[]{:S(2)}) collective-permute-start(bf16[2,96,2,128]{3,1,2,0:T(8,128)(2,1)} %get-tuple-element.263), channel_id=1, source_target_pairs={{0,5},{1,4},{2,7},{3,6},{4,1},{5,0},{6,3},{7,2},{8,13},{9,12},{10,... | collective-permute-start | bytes 294920 | tf_op jit(solution)/shard_map/ppermute | solution.py:29
  10.4 9.7 %all-to-all-start.5 = ((bf16[16,2,32]{2,1,0:T(2,128)(2,1)}), bf16[16,2,32]{2,1,0:T(2,128)(2,1)S(1)}, u32[]{:S(2)}, u32[]{:S(2)}) async-start(bf16[16,2,32]{2,1,0:T(2,128)(2,1)} %broadcast_in_dim.91), calls=%async_computation.5 | async-start | bytes 16384 | tf_op jit(solution)/shard_map/all_to_all | solution.py:132
  20.7 21.4 %all-to-all-start.3 = ((bf16[16,4,32]{2,1,0:T(4,128)(2,1)}), bf16[16,4,32]{2,1,0:T(4,128)(2,1)S(1)}, u32[]{:S(2)}, u32[]{:S(2)}) async-start(bf16[16,4,32]{2,1,0:T(4,128)(2,1)} %broadcast_in_dim.90), calls=%async_computation.3 | async-start | bytes 32768 | tf_op jit(solution)/shard_map/all_to_all | solution.py:126
  42.2 29.3 %copy-start.15 = (bf16[2,96,2,128]{3,1,2,0:T(8,128)(2,1)S(1)}, bf16[2,96,2,128]{3,1,2,0:T(8,128)(2,1)}, u32[]{:S(2)}) copy-start(bf16[2,96,2,128]{3,1,2,0:T(8,128)(2,1)} %get-tuple-element.258) | copy-start | bytes 294916
  42.2 36.4 %copy-start.14 = (bf16[2,96,2,128]{3,1,2,0:T(8,128)(2,1)S(1)}, bf16[2,96,2,128]{3,1,2,0:T(8,128)(2,1)}, u32[]{:S(2)}) copy-start(bf16[2,96,2,128]{3,1,2,0:T(8,128)(2,1)} %get-tuple-element.257) | copy-start | bytes 294916
  42.2 14.2 %all-to-all-start.7 = ((bf16[32,32,128]{2,1,0:T(8,128)(2,1)}), bf16[32,32,128]{2,1,0:T(8,128)(2,1)S(1)}, u32[]{:S(2)}, u32[]{:S(2)}) async-start(bf16[32,32,128]{2,1,0:T(8,128)(2,1)} %bitcast.53), calls=%async_computation.7 | async-start | bytes 524288 | tf_op jit(solution)/shard_map/all_to_all | solution.py:130
  56.4 25.7 %all-to-all-start.6 = ((bf16[32,32,3,128]{3,1,2,0:T(8,128)(2,1)}), bf16[32,32,3,128]{3,1,2,0:T(8,128)(2,1)S(1)}, u32[]{:S(2)}, u32[]{:S(2)}) async-start(bf16[32,32,3,128]{3,1,2,0:T(8,128)(2,1)} %bitcast.48), calls=%async_computation.6 | async-start | bytes 1572864 | tf_op jit(solution)/shard_map/all_to_all | solution.py:129
  62.2 16.4 %collective-permute-start.5 = (bf16[2,96,2,128]{3,1,2,0:T(8,128)(2,1)}, bf16[2,96,2,128]{3,1,2,0:T(8,128)(2,1)S(1)}, u32[]{:S(2)}, u32[]{:S(2)}) collective-permute-start(bf16[2,96,2,128]{3,1,2,0:T(8,128)(2,1)} %get-tuple-element.262), channel_id=1, source_target_pairs={{0,6},{1,7},{2,4},{3,5},{4,2},{5,3},{6,0},{7,1},{8,14},{9,15},{10,... | collective-permute-start | bytes 294920 | tf_op jit(solution)/shard_map/ppermute | solution.py:29
  63.2 31.6 %copy-start.13 = (bf16[2,96,2,128]{3,1,2,0:T(8,128)(2,1)S(1)}, bf16[2,96,2,128]{3,1,2,0:T(8,128)(2,1)}, u32[]{:S(2)}) copy-start(bf16[2,96,2,128]{3,1,2,0:T(8,128)(2,1)} %get-tuple-element.256) | copy-start | bytes 294916
  63.2 31.5 %collective-permute-start.6 = (bf16[2,96,2,128]{3,1,2,0:T(8,128)(2,1)}, bf16[2,96,2,128]{3,1,2,0:T(8,128)(2,1)}, u32[]{:S(2)}, u32[]{:S(2)}) collective-permute-start(bf16[2,96,2,128]{3,1,2,0:T(8,128)(2,1)} %get-tuple-element.261), channel_id=1, source_target_pairs={{0,7},{1,6},{2,5},{3,4},{4,3},{5,2},{6,1},{7,0},{8,15},{9,14},{10,... | collective-permute-start | bytes 294920 | tf_op jit(solution)/shard_map/ppermute | solution.py:29
  67.0 29.9 %copy-start.12 = (bf16[2,96,2,128]{3,1,2,0:T(8,128)(2,1)S(1)}, bf16[2,96,2,128]{3,1,2,0:T(8,128)(2,1)}, u32[]{:S(2)}) copy-start(bf16[2,96,2,128]{3,1,2,0:T(8,128)(2,1)} %get-tuple-element.255) | copy-start | bytes 294916
  67.1 29.9 %collective-permute-start.7 = (bf16[2,96,2,128]{3,1,2,0:T(8,128)(2,1)S(1)}, bf16[2,96,2,128]{3,1,2,0:T(8,128)(2,1)}, u32[]{:S(2)}, u32[]{:S(2)}) collective-permute-start(bf16[2,96,2,128]{3,1,2,0:T(8,128)(2,1)S(1)} %copy-done.17), channel_id=1, source_target_pairs={{0,8},{1,9},{2,10},{3,11},{4,12},{5,13},{6,14},{7,15},{8,0},{9,1},... | collective-permute-start | bytes 294920 | tf_op jit(solution)/shard_map/ppermute | solution.py:29
  70.2 28.6 %copy-start.11 = (bf16[2,96,2,128]{3,1,2,0:T(8,128)(2,1)S(1)}, bf16[2,96,2,128]{3,1,2,0:T(8,128)(2,1)}, u32[]{:S(2)}) copy-start(bf16[2,96,2,128]{3,1,2,0:T(8,128)(2,1)} %get-tuple-element.254) | copy-start | bytes 294916
  70.2 28.5 %collective-permute-start.8 = (bf16[2,96,2,128]{3,1,2,0:T(8,128)(2,1)S(1)}, bf16[2,96,2,128]{3,1,2,0:T(8,128)(2,1)}, u32[]{:S(2)}, u32[]{:S(2)}) collective-permute-start(bf16[2,96,2,128]{3,1,2,0:T(8,128)(2,1)S(1)} %copy-done.16), channel_id=1, source_target_pairs={{0,9},{1,8},{2,11},{3,10},{4,13},{5,12},{6,15},{7,14},{8,1},{9,0},... | collective-permute-start | bytes 294920 | tf_op jit(solution)/shard_map/ppermute | solution.py:29
  71.5 29.5 %copy-start.10 = (bf16[2,96,2,128]{3,1,2,0:T(8,128)(2,1)S(1)}, bf16[2,96,2,128]{3,1,2,0:T(8,128)(2,1)}, u32[]{:S(2)}) copy-start(bf16[2,96,2,128]{3,1,2,0:T(8,128)(2,1)} %get-tuple-element.253) | copy-start | bytes 294916
  71.5 29.5 %collective-permute-start.9 = (bf16[2,96,2,128]{3,1,2,0:T(8,128)(2,1)S(1)}, bf16[2,96,2,128]{3,1,2,0:T(8,128)(2,1)}, u32[]{:S(2)}, u32[]{:S(2)}) collective-permute-start(bf16[2,96,2,128]{3,1,2,0:T(8,128)(2,1)S(1)} %copy-done.15), channel_id=1, source_target_pairs={{0,10},{1,11},{2,8},{3,9},{4,14},{5,15},{6,12},{7,13},{8,2},{9,3},... | collective-permute-start | bytes 294920 | tf_op jit(solution)/shard_map/ppermute | solution.py:29
  78.6 24.5 %collective-permute-start.10 = (bf16[2,96,2,128]{3,1,2,0:T(8,128)(2,1)S(1)}, bf16[2,96,2,128]{3,1,2,0:T(8,128)(2,1)}, u32[]{:S(2)}, u32[]{:S(2)}) collective-permute-start(bf16[2,96,2,128]{3,1,2,0:T(8,128)(2,1)S(1)} %copy-done.14), channel_id=1, source_target_pairs={{0,11},{1,10},{2,9},{3,8},{4,15},{5,14},{6,13},{7,12},{8,3},{9,2},... | collective-permute-start | bytes 294920 | tf_op jit(solution)/shard_map/ppermute | solution.py:29
  82.1 49.0 %copy-start.2 = (bf16[32,32,3,128]{3,1,2,0:T(8,128)(2,1)}, bf16[32,32,3,128]{3,1,2,0:T(8,128)(2,1)S(1)}, u32[]{:S(2)}) copy-start(bf16[32,32,3,128]{3,1,2,0:T(8,128)(2,1)S(1)} %all-to-all-done.6) | copy-start | bytes 2359300
  82.1 57.3 %all-to-all-start.2 = ((bf16[64,32,2,128]{3,1,2,0:T(8,128)(2,1)}), bf16[64,32,2,128]{3,1,2,0:T(8,128)(2,1)}, u32[]{:S(2)}, u32[]{:S(2)}) async-start(bf16[64,32,2,128]{3,1,2,0:T(8,128)(2,1)} %bitcast.36), calls=%async_computation.2 | async-start | bytes 2097152 | tf_op jit(solution)/shard_map/all_to_all | solution.py:125
  94.8 36.3 %collective-permute-start.11 = (bf16[2,96,2,128]{3,1,2,0:T(8,128)(2,1)S(1)}, bf16[2,96,2,128]{3,1,2,0:T(8,128)(2,1)S(1)}, u32[]{:S(2)}, u32[]{:S(2)}) collective-permute-start(bf16[2,96,2,128]{3,1,2,0:T(8,128)(2,1)S(1)} %copy-done.13), channel_id=1, source_target_pairs={{0,12},{1,13},{2,14},{3,15},{4,8},{5,9},{6,10},{7,11},{8,4},{9,5},... | collective-permute-start | bytes 294920 | tf_op jit(solution)/shard_map/ppermute | solution.py:29
  96.9 37.2 %collective-permute-start.12 = (bf16[2,96,2,128]{3,1,2,0:T(8,128)(2,1)S(1)}, bf16[2,96,2,128]{3,1,2,0:T(8,128)(2,1)S(1)}, u32[]{:S(2)}, u32[]{:S(2)}) collective-permute-start(bf16[2,96,2,128]{3,1,2,0:T(8,128)(2,1)S(1)} %copy-done.12), channel_id=1, source_target_pairs={{0,13},{1,12},{2,15},{3,14},{4,9},{5,8},{6,11},{7,10},{8,5},{9,4},... | collective-permute-start | bytes 294920 | tf_op jit(solution)/shard_map/ppermute | solution.py:29
  98.7 36.5 %collective-permute-start.13 = (bf16[2,96,2,128]{3,1,2,0:T(8,128)(2,1)S(1)}, bf16[2,96,2,128]{3,1,2,0:T(8,128)(2,1)S(1)}, u32[]{:S(2)}, u32[]{:S(2)}) collective-permute-start(bf16[2,96,2,128]{3,1,2,0:T(8,128)(2,1)S(1)} %copy-done.11), channel_id=1, source_target_pairs={{0,14},{1,15},{2,12},{3,13},{4,10},{5,11},{6,8},{7,9},{8,6},{9,7},... | collective-permute-start | bytes 294920 | tf_op jit(solution)/shard_map/ppermute | solution.py:29
  101.0 36.6 %collective-permute-start.14 = (bf16[2,96,2,128]{3,1,2,0:T(8,128)(2,1)S(1)}, bf16[2,96,2,128]{3,1,2,0:T(8,128)(2,1)S(1)}, u32[]{:S(2)}, u32[]{:S(2)}) collective-permute-start(bf16[2,96,2,128]{3,1,2,0:T(8,128)(2,1)S(1)} %copy-done.10), channel_id=1, source_target_pairs={{0,15},{1,14},{2,13},{3,12},{4,11},{5,10},{6,9},{7,8},{8,7},{9,6},... | collective-permute-start | bytes 294920 | tf_op jit(solution)/shard_map/ppermute | solution.py:29
  139.4 40.3 %all-to-all-start.1 = ((bf16[64,96,128]{2,1,0:T(8,128)(2,1)}), bf16[64,96,128]{2,1,0:T(8,128)(2,1)S(1)}, u32[]{:S(2)}, u32[]{:S(2)}) async-start(bf16[64,96,128]{2,1,0:T(8,128)(2,1)} %bitcast.30), calls=%async_computation.1 | async-start | bytes 3145728 | tf_op jit(solution)/shard_map/all_to_all | solution.py:124
  179.7 109.2 %all-to-all-start = ((bf16[64,96,3,128]{3,1,2,0:T(8,128)(2,1)}), bf16[64,96,3,128]{3,1,2,0:T(8,128)(2,1)}, u32[]{:S(2)}, u32[]{:S(2)}) async-start(bf16[64,96,3,128]{3,1,2,0:T(8,128)(2,1)} %bitcast.290), calls=%async_computation | async-start | bytes 9437184 | tf_op jit(solution)/shard_map/all_to_all | solution.py:123
  288.9 50.6 %all-to-all-start.8 = ((bf16[2,512,128]{2,0,1:T(2,128)(2,1)}), bf16[2,512,128]{2,0,1:T(2,128)(2,1)}, u32[]{:S(2)}, u32[]{:S(2)}) async-start(bf16[2,512,128]{2,0,1:T(2,128)(2,1)} %copy.100), calls=%async_computation.8 | async-start | bytes 524288 | tf_op jit(solution)/shard_map/all_to_all | solution.py:153
  299.7 29.7 %copy-start.18 = (f32[4,128]{1,0:T(4,128)S(1)}, f32[4,128]{1,0:T(4,128)}, u32[]{:S(2)}) copy-start(f32[4,128]{1,0:T(4,128)} %constant_dynamic-slice_fusion.2) | copy-start | bytes 6148
  339.5 42.2 %all-to-all-start.4 = ((bf16[4,1536,128]{2,0,1:T(4,128)(2,1)}), bf16[4,1536,128]{2,0,1:T(4,128)(2,1)S(1)}, u32[]{:S(2)}, u32[]{:S(2)}) async-start(bf16[4,1536,128]{2,0,1:T(4,128)(2,1)} %copy.88), calls=%async_computation.4 | async-start | bytes 3145728 | tf_op jit(solution)/shard_map/all_to_all | solution.py:152
  (16 other events, 140.1 us)
